TPU v7x, 128 devices: a whole 4x4x4 slice. The times are simulated.
128 devices in a mesh: gx: 8 (over z, core), gy: 16 (over y, x).
Axes of the slice: x: 4, y: 4, z: 4, core: 2. Of those that a mesh axis runs over, the one named last changes fastest.
Arguments:
- tiles: bfloat16 [24576, 128, 128], P(('gx', 'gy')), may hold values from -6 to 6
- tile_rows: int32 [24576], P(('gx', 'gy')), may hold values from 0 to 63, as said below
- tile_cols: int32 [24576], P(('gx', 'gy')), may hold values from 0 to 255
- tile_counts: int32 [128], P(('gx', 'gy')), may hold values from 48 to 192
- block_order: int32 [256], replicated, may hold values from 0 to 255, each once
- sketch: bfloat16 [32768, 128], replicated, may hold values from -6 to 6
Outputs:
- cell_factor: bfloat16 [1048576, 128], P(('gx', 'gy'))
- gene_factor: float32 [32768, 128], P(('gx', 'gy'))
Inputs may be any that keep to these rules, and one draw needn't show every extreme that they name: On each device the live slots (those below its count) hold distinct coordinate pairs (tile_rows, tile_cols) in increasing lexicographic order; later slots are unused. `block_order`: device d along gx+gy owns the gene blocks in entries d * 2 to (d + 1) * 2 - 1.
All inputs are finite; a program needn't handle non-finite values.
Results may differ from a plain program's by a relative error of at most 0.0019.
Values sent between devices are 32-bit elements; how exact they have to be, the bound alone decides.
A program may use at most 192 MiB of HBM per device.

v0:
```python
import math
import jax
import jax.numpy as jnp
from jax import lax
from jax.sharding import PartitionSpec as P

TILE = 128
SKETCH = 128
GENES = 32768
CB_DEV = 64


def on_device(tiles, tile_rows, tile_cols, tile_counts, block_order, sketch):
    live_count = tile_counts[0]
    blocks_total = GENES // TILE
    sketch_blocks = sketch.reshape(blocks_total, TILE, SKETCH)
    width = 16
    turns = (live_count + width - 1) // width

    def take(start):
        tile_block = lax.dynamic_slice_in_dim(tiles, start, width, 0)
        row_block = lax.dynamic_slice_in_dim(tile_rows, start, width, 0)
        col_block = lax.dynamic_slice_in_dim(tile_cols, start, width, 0)
        alive = start + jnp.arange(width, dtype=jnp.int32) < live_count
        return (tile_block, row_block, col_block, alive)

    def cell_step(turn, total):
        tile_block, row_block, col_block, alive = take(turn * width)
        product = jnp.einsum(
            "tij,tjs->tis", tile_block, sketch_blocks[col_block], preferred_element_type=jnp.float32
        )
        product = jnp.where(alive[:, None, None], product, 0.0)
        return total.at[row_block].add(product)

    cell_sum = lax.fori_loop(0, turns, cell_step, jnp.zeros((CB_DEV, TILE, SKETCH), jnp.float32))
    cell_sum = cell_sum.reshape(CB_DEV * TILE, SKETCH)
    local_gram = jnp.dot(
        cell_sum.T, cell_sum, precision=lax.Precision.HIGHEST, preferred_element_type=jnp.float32
    )
    gram = lax.psum(local_gram, ("gx", "gy"))
    cells_all = CB_DEV * TILE * lax.axis_size("gx") * lax.axis_size("gy")
    lower = jnp.linalg.cholesky(gram)
    cell_factor = (
        math.sqrt(cells_all)
        * lax.linalg.triangular_solve(
            lower, cell_sum, left_side=False, lower=True, transpose_a=True
        )
    ).astype(jnp.bfloat16)
    cell_blocks = cell_factor.reshape(CB_DEV, TILE, SKETCH)

    def gene_step(turn, total):
        tile_block, row_block, col_block, alive = take(turn * width)
        product = jnp.einsum(
            "tji,tjs->tis", tile_block, cell_blocks[row_block], preferred_element_type=jnp.float32
        )
        product = jnp.where(alive[:, None, None], product, 0.0)
        return total.at[col_block].add(product)

    gene_sum = lax.fori_loop(
        0, turns, gene_step, jnp.zeros((blocks_total, TILE, SKETCH), jnp.float32)
    )
    ordered = gene_sum[block_order].reshape(GENES, SKETCH)
    owned = lax.psum_scatter(ordered, ("gx", "gy"), scatter_dimension=0, tiled=True)
    gene_gram = lax.psum(
        jnp.dot(
            owned.T, owned, precision=lax.Precision.HIGHEST, preferred_element_type=jnp.float32
        ),
        ("gx", "gy"),
    )
    lower_genes = jnp.linalg.cholesky(gene_gram)
    gene_factor = math.sqrt(GENES) * lax.linalg.triangular_solve(
        lower_genes, owned, left_side=False, lower=True, transpose_a=True
    )
    return (cell_factor, gene_factor)


def solution(mesh):
    placed = (
        P(("gx", "gy"), None, None),
        P(("gx", "gy")),
        P(("gx", "gy")),
        P(("gx", "gy")),
        P(),
        P(),
    )
    return jax.shard_map(
        on_device,
        mesh=mesh,
        in_specs=placed,
        out_specs=(P(("gx", "gy"), None), P(("gx", "gy"), None)),
        check_vma=False,
    )
```

profile of v0, /device:TPU:1, one launch (start us, length us, event | category | flops | bytes accessed | tf_op | source)
XLA Modules:
  0.0 1278.8 jit_solution(311369099258729333)
XLA Ops:
  10.3 47.0 %while.20 = (s32[]{:T(128)}, f32[64,128,128]{2,1,0:T(8,128)}, s32[]{:T(128)}, s32[192]{0:T(256)S(1)}, s32[]{:T(128)}, /*index=5*/bf16[192,128,128]{2,1,0:T(8,128...) while((s32[]{:T(128)}, f32[64,128,128]{2,1,0:T(8,128)}, ...), condition=%wide.region_2.3_spmd, body=%wide.region_0.2_spmd.sunk | while | flops 67634312 | bytes 6296211 | solution.py:35
  10.4 4.0 gather_fusion
  16.5 3.4 scatter_fusion
  19.9 4.0 gather_fusion
  29.3 4.0 gather_fusion
  38.6 4.0 gather_fusion
  48.0 4.0 gather_fusion
  57.4 10.8 convolution_bitcast_fusion
  68.5 208.9 %all-reduce.3.cloned.1.call-done = f32[128,128]{0,1:T(8,128)} async-done(((f32[128,128]{0,1:T(8,128)}), f32[128,128]{0,1:T(8,128)}) %all-reduce.3.cloned.1.call-update) | async-done | bytes 65552 | tf_op jit(solution)/shard_map/psum | solution.py:40
  279.2 11.7 cholesky.44
  292.2 9.8 custom-call.8
  302.0 6.2 fusion.4
  308.2 7.8 broadcast_in_dim.45
  316.0 39.0 %while.21 = (s32[]{:T(128)}, f32[256,128,128]{2,1,0:T(8,128)}, s32[]{:T(128)}, s32[192]{0:T(256)S(1)}, s32[]{:T(128)}, /*index=5*/bf16[192,128,128]{2,1,0:T(8,12...) while((s32[]{:T(128)}, f32[256,128,128]{2,1,0:T(8,128)}, ...), condition=%wide.region_8.10_spmd, body=%wide.region_6.9_spmd.sunk | while | flops 67634312 | bytes 6296211 | solution.py:59
  320.4 3.4 scatter_fusion.1
  328.2 3.4 scatter_fusion.1
  336.0 3.4 scatter_fusion.1
  343.8 3.4 scatter_fusion.1
  351.6 3.4 scatter_fusion.1
  355.0 17.7 %gather_fusion.2 = f32[256,128,128]{2,1,0:T(8,128)} fusion(f32[256,128,128]{2,1,0:T(8,128)} %get-tuple-element.90, s32[1024]{0:T(1024)S(1)} %pad_clamp_fusion.2), kind=kCustom, calls=%fused_computation.2 | custom fusion | bytes 33555456 | tf_op jit(solution)/shard_map/gather | solution.py:62
  372.7 702.3 %reduce-scatter.2.cloned.1.call-done = f32[256,128]{1,0:T(8,128)} async-done(((f32[32768,128]{1,0:T(8,128)}), f32[256,128]{1,0:T(8,128)}) %reduce-scatter.2.cloned.1.call-update) | async-done | bytes 131088 | tf_op jit(solution)/shard_map/reduce_scatter | solution.py:63
  1077.0 168.8 %all-reduce.5.cloned.1.call-done = f32[128,128]{0,1:T(8,128)} async-done(((f32[128,128]{0,1:T(8,128)}), f32[128,128]{0,1:T(8,128)}) %all-reduce.5.cloned.1.call-update) | async-done | bytes 65552 | tf_op jit(solution)/shard_map/psum | solution.py:64
  1247.6 11.7 cholesky.55
  1260.7 9.8 custom-call.9
  (76 shorter events, 58.1 us)
Async XLA Ops:
  7.2 3.2 copy-start
  7.2 3.2 copy-start.1
  7.2 270.2 %all-reduce.3.cloned.1.call-start = ((), (), s32[]{:S(2)}) async-start(), calls=%async_computation.1 | async-start | bytes 131072 | tf_op jit(solution)/shard_map/psum | solution.py:40
  57.4 11.1 copy-start.2
  68.2 1006.8 %reduce-scatter.2.cloned.1.call-start = ((), (), s32[]{:S(2)}) async-start(), calls=%async_computation.2 | async-start | bytes 16908288 | tf_op jit(solution)/shard_map/reduce_scatter | solution.py:63
  372.7 873.2 %all-reduce.5.cloned.1.call-start = ((), (), s32[]{:S(2)}) async-start(), calls=%async_computation.3 | async-start | bytes 131072 | tf_op jit(solution)/shard_map/psum | solution.py:64
Sparse Core Ops, SparseCore 0:
  68.3 208.9 all-reduce.2
  372.8 702.1 reduce-scatter.1
  1080.3 165.4 all-reduce.4
where the time goes:
time: 1280 us
  waiting for transfers between devices  1080 us (84%)
  other arithmetic  88.2 us (7%)
  local copies, waits for them, and re-layouts  61.1 us (5%)
  matrix products  34.5 us (3%)
  between operations  14.5 us (1%)
    reduce_scatter x1, waiting for transfers between devices, on_device(): lax.psum_scatter(ordered, ('gx', 'gy'), scatter_dimension=0, tiled=True)  702 us
    psum x1, waiting for transfers between devices, on_device(): gram = lax.psum(local_gram, ('gx', 'gy'))  209 us
    psum x1, waiting for transfers between devices, on_device(): lax.psum(jnp.dot(owned.T, owned, precision=lax.Precision.HIGHEST, preferr...  169 us
  transfers between devices with their start and end apart: 3, of which 3 were waited for; matrix products, arithmetic and copies ran while one was open for 0% of the time, Pallas kernels for 0%

commit v1 on v0

--- a/solution.py
+++ b/solution.py
@@ -37,7 +37,7 @@
     local_gram = jnp.dot(
         cell_sum.T, cell_sum, precision=lax.Precision.HIGHEST, preferred_element_type=jnp.float32
     )
-    gram = lax.psum(local_gram, ("gx", "gy"))
+    gram = jnp.sum(lax.all_gather(local_gram, ("gx", "gy")), axis=0)
     cells_all = CB_DEV * TILE * lax.axis_size("gx") * lax.axis_size("gy")
     lower = jnp.linalg.cholesky(gram)
     cell_factor = (

time: 1280 us -> 1220 us (0.953)
  waiting for transfers between devices: 1080 us -> 1010 us
    psum x1 -> x0, waiting for transfers between devices: 209 us -> none  [on_device(): gram = lax.psum(local_gram, ('gx', 'gy'))]
    all_gather x0 -> x1, waiting for transfers between devices: none -> 140 us  [on_device(): gram = jnp.sum(lax.all_gather(local_gram, ('gx', 'gy')), axis=0)]
where the time goes in v1:
time: 1220 us; the launch traced here: 1210 us
  waiting for transfers between devices  1010 us (83%)
  other arithmetic  91.1 us (7%)
  local copies, waits for them, and re-layouts  60.4 us (5%)
  matrix products  34.5 us (3%)
  between operations  14.5 us (1%)
    reduce_scatter x1, waiting for transfers between devices, on_device(): lax.psum_scatter(ordered, ('gx', 'gy'), scatter_dimension=0, tiled=True)  703 us
    psum x1, waiting for transfers between devices, on_device(): lax.psum(jnp.dot(owned.T, owned, precision=lax.Precision.HIGHEST, preferr...  169 us
    all_gather x1, waiting for transfers between devices, on_device(): gram = jnp.sum(lax.all_gather(local_gram, ('gx', 'gy')), axis=0)  140 us
  transfers between devices with their start and end apart: 3, of which 3 were waited for; matrix products, arithmetic and copies ran while one was open for 0% of the time, Pallas kernels for 0%

profile of v1, /device:TPU:1, one launch (start us, length us, event | category | flops | bytes accessed | tf_op | source)
XLA Modules:
  0.0 1213.1 jit_solution(5570681264958211143)
XLA Ops:
  10.4 47.0 %while.20 = (s32[]{:T(128)}, f32[64,128,128]{2,1,0:T(8,128)}, s32[]{:T(128)}, s32[192]{0:T(256)S(1)}, s32[]{:T(128)}, /*index=5*/bf16[192,128,128]{2,1,0:T(8,128...) while((s32[]{:T(128)}, f32[64,128,128]{2,1,0:T(8,128)}, ...), condition=%wide.region_2.3_spmd, body=%wide.region_0.2_spmd.sunk | while | flops 67634312 | bytes 6296211 | solution.py:35
  10.5 4.0 gather_fusion
  19.9 4.0 gather_fusion
  29.3 4.0 gather_fusion
  38.6 4.0 gather_fusion
  48.1 4.0 gather_fusion
  57.4 10.8 convolution_bitcast_fusion
  68.5 139.9 %all-gather.3.cloned.1.call-done = f32[16384,128]{1,0:T(8,128)} async-done(((f32[128,128]{1,0:T(8,128)}), f32[16384,128]{1,0:T(8,128)}) %all-gather.3.cloned.1.call-update) | async-done | bytes 8388624 | tf_op jit(solution)/shard_map/all_gather | solution.py:40
  208.5 3.8 reduce_sum.9
  212.4 11.7 cholesky.44
  225.4 9.8 custom-call.8
  235.3 6.2 fusion.4
  241.4 7.8 broadcast_in_dim.45
  249.3 39.0 %while.21 = (s32[]{:T(128)}, f32[256,128,128]{2,1,0:T(8,128)}, s32[]{:T(128)}, s32[192]{0:T(256)S(1)}, s32[]{:T(128)}, /*index=5*/bf16[192,128,128]{2,1,0:T(8,12...) while((s32[]{:T(128)}, f32[256,128,128]{2,1,0:T(8,128)}, ...), condition=%wide.region_8.10_spmd, body=%wide.region_6.9_spmd.sunk | while | flops 67634312 | bytes 6296211 | solution.py:59
  253.7 3.4 scatter_fusion.1
  261.5 3.4 scatter_fusion.1
  269.3 3.4 scatter_fusion.1
  277.0 3.4 scatter_fusion.1
  284.8 3.4 scatter_fusion.1
  288.2 17.7 %gather_fusion.2 = f32[256,128,128]{2,1,0:T(8,128)} fusion(f32[256,128,128]{2,1,0:T(8,128)} %get-tuple-element.90, s32[1024]{0:T(1024)S(1)} %pad_clamp_fusion.2), kind=kCustom, calls=%fused_computation.2 | custom fusion | bytes 33555456 | tf_op jit(solution)/shard_map/gather | solution.py:62
  306.0 703.1 %reduce-scatter.2.cloned.1.call-done = f32[256,128]{1,0:T(8,128)} async-done(((f32[32768,128]{1,0:T(8,128)}), f32[256,128]{1,0:T(8,128)}) %reduce-scatter.2.cloned.1.call-update) | async-done | bytes 131088 | tf_op jit(solution)/shard_map/reduce_scatter | solution.py:63
  1011.1 169.0 %all-reduce.2.cloned.1.call-done = f32[128,128]{0,1:T(8,128)} async-done(((f32[128,128]{0,1:T(8,128)}), f32[128,128]{0,1:T(8,128)}) %all-reduce.2.cloned.1.call-update) | async-done | bytes 65552 | tf_op jit(solution)/shard_map/psum | solution.py:64
  1181.9 11.7 cholesky.55
  1195.0 9.8 custom-call.9
  (77 shorter events, 59.8 us)
Async XLA Ops:
  7.2 3.2 copy-start
  7.2 3.2 copy-start.1
  7.2 201.3 %all-gather.3.cloned.1.call-start = ((), (), s32[]{:S(2)}) async-start(), calls=%async_computation.3 | async-start | bytes 8454144 | tf_op jit(solution)/shard_map/all_gather | solution.py:40
  57.4 11.1 copy-start.2
  68.3 940.8 %reduce-scatter.2.cloned.1.call-start = ((), (), s32[]{:S(2)}) async-start(), calls=%async_computation.1 | async-start | bytes 16908288 | tf_op jit(solution)/shard_map/reduce_scatter | solution.py:63
  305.9 874.2 %all-reduce.2.cloned.1.call-start = ((), (), s32[]{:S(2)}) async-start(), calls=%async_computation.2 | async-start | bytes 131072 | tf_op jit(solution)/shard_map/psum | solution.py:64
Sparse Core Ops, SparseCore 0:
  68.4 140.0 all-gather.2
  306.0 703.0 reduce-scatter.1
  1014.4 165.6 all-reduce.1
